TPU v7x, 32 devices: a whole 2x2x4 slice. The times are simulated.
32 devices in a mesh: dp: 8 (over z, x), mlp: 4 (over y, core).
Axes of the slice: x: 2, y: 2, z: 4, core: 2. Of those that a mesh axis runs over, the one named last changes fastest.
Arguments:
- tokens: bfloat16 [32768, 768], P(('dp', 'mlp')), may hold values from -6 to 6
- cotangent: bfloat16 [32768, 768], P(('dp', 'mlp')), may hold values from -6 to 6
- vectors: float32 [14, 768], replicated
- vector_moments: float32 [14, 768], replicated, may hold values from 819.2 to 26214.4
- decays: float32 [2], replicated, may hold values from 0.9 to 0.98
- owner: int32 [4, 3], replicated, may hold values from 0 to 7, as said below
- master_slots: float32 [8, 4, 768, 768], P('dp', 'mlp'), as said below
- left_slots: float32 [8, 4, 768, 768], P('dp', 'mlp'), as said below
- right_slots: float32 [8, 4, 768, 768], P('dp', 'mlp'), as said below
- left_roots: float32 [8, 4, 768, 768], P('dp', 'mlp'), as said below
- right_roots: float32 [8, 4, 768, 768], P('dp', 'mlp'), as said below
- grid_height: int32 [128], P(('dp', 'mlp')), may hold values from 8 to 24, as said below
- grid_width: int32 [128], P(('dp', 'mlp')), may hold values from 8 to 24, as said below
- patch_rows: int32 [32768], P(('dp', 'mlp')), may hold values from 0 to 23, as said below
- patch_cols: int32 [32768], P(('dp', 'mlp')), may hold values from 0 to 23, as said below
- segment: int32 [32768], P(('dp', 'mlp')), may hold values from 0 to 3, as said below
Outputs:
- output: bfloat16 [32768, 768], P(('dp', 'mlp'))
- input_grad: float32 [32768, 768], P(('dp', 'mlp'))
- slot_grads: float32 [8, 4, 768, 768], P('dp', 'mlp')
- new_left: float32 [8, 4, 768, 768], P('dp', 'mlp')
- new_right: float32 [8, 4, 768, 768], P('dp', 'mlp')
- new_master: float32 [8, 4, 768, 768], P('dp', 'mlp')
- vector_grads: float32 [14, 768], P(None, 'mlp')
- new_vector_moments: float32 [14, 768], P(None, 'mlp')
- new_vectors: float32 [14, 768], P(None, 'mlp')
Inputs may be any that keep to these rules, and one draw needn't show every extreme that they name: `owner`: the entries of a row differ; block kind 0 of row m is the m-th of the query, key, value and output projections, kind 1 the m-th 768 columns of the up projection, kind 2 the m-th 768 rows of the down projection. `master_slots`: slot (owner[m,k], m) holds block kind k of row m; the other slots are unused. `left_slots`: symmetric and positive definite. `right_slots`: symmetric and positive definite. `left_roots`: symmetric and positive definite. `right_roots`: symmetric and positive definite. `grid_height`: each image is 16 patches along one side; the other sides of one device's images add up to 64. `grid_width`: as grid_height. `patch_rows`: each device's patches hold its images whole, one after another in the order of their numbers, each in raster order. `patch_cols`: as patch_rows. `segment`: never falls within a device's patches.
All inputs are finite; a program needn't handle non-finite values.
Results may differ from a plain program's by a relative error of at most 0.014.
Values may be sent and summed in bfloat16 or wider, within the bound.
A program may use at most 192 MiB of HBM per device.

v0:
```python
import math
import jax
import jax.numpy as jnp
from jax import lax
from jax.sharding import PartitionSpec as P

HEADS = 12
GRID_BASE = 16
NORM_EPSILON = 1e-06
GRAFT_EPSILON = 1e-06
STEP_EPSILON = 1e-08
RATE_MATRIX = 0.04
RATE_VECTOR = 0.02
MASKED_SCORE = -1e30


def layer_norm(values, gain_row, shift_row):
    centred = values - jnp.mean(values, axis=-1, keepdims=True)
    spread = jnp.mean(centred * centred, axis=-1, keepdims=True)
    return centred * lax.rsqrt(spread + NORM_EPSILON) * gain_row + shift_row


def exact_gelu(values):
    return jax.nn.gelu(values, approximate=False)


def rotate_pairs(flat_values, freq_row, rows_pos, cols_pos):
    tokens_here = flat_values.shape[0]
    values = flat_values.reshape(tokens_here, HEADS, -1)
    half_size = values.shape[-1] // 2
    middle = freq_row.shape[0] // 2
    freq_cols = freq_row[:middle].reshape(HEADS, half_size)
    freq_rows = freq_row[middle:].reshape(HEADS, half_size)
    angle_grid = (
        rows_pos[:, None, None] * freq_rows[None] + cols_pos[:, None, None] * freq_cols[None]
    )
    cosine = jnp.cos(angle_grid)
    sine_part = jnp.sin(angle_grid)
    first_half = values[..., :half_size]
    second = values[..., half_size:]
    turned = jnp.concatenate(
        [first_half * cosine - second * sine_part, second * cosine + first_half * sine_part],
        axis=-1,
    )
    return turned.reshape(tokens_here, -1)


def patch_positions(segment_ids, heights_in, widths_in, rows_in, cols_in):
    images_here = heights_in.shape[0]
    matches = segment_ids[:, None] == jnp.arange(images_here, dtype=jnp.int32)[None, :]
    heights = jnp.sum(jnp.where(matches, heights_in[None, :], 0), axis=1).astype(jnp.float32)
    widths = jnp.sum(jnp.where(matches, widths_in[None, :], 0), axis=1).astype(jnp.float32)
    rows_pos = rows_in.astype(jnp.float32) * GRID_BASE / heights
    cols_pos = cols_in.astype(jnp.float32) * GRID_BASE / widths
    return (rows_pos, cols_pos)


def heads_first(flat_values):
    return jnp.swapaxes(flat_values.reshape(flat_values.shape[0], HEADS, -1), 0, 1)


def tokens_first(stacked):
    return jnp.swapaxes(stacked, 0, 1).reshape(stacked.shape[1], -1)


def local(
    tokens,
    cotangent,
    vectors,
    vector_moments,
    decays,
    owner,
    master_slots,
    left_slots,
    right_slots,
    left_roots,
    right_roots,
    grid_height,
    grid_width,
    patch_rows,
    patch_cols,
    segment,
):
    dp_index = lax.axis_index("dp")
    mlp_index = lax.axis_index("mlp")
    groups_mlp = lax.axis_size("mlp")
    model_width = tokens.shape[1]
    rows_here = tokens.shape[0]
    owner_row = jnp.take(owner, mlp_index, axis=0)
    holds_block = owner_row == dp_index
    owned_blocks = jnp.where(holds_block[:, None, None], master_slots[0, 0][None], 0.0)
    blocks = lax.psum(owned_blocks, "dp")
    blocks_low = blocks.astype(jnp.bfloat16)
    up_rows = vectors[8 : 8 + groups_mlp]
    down_bias = vectors[8 + groups_mlp]
    freq_row = vectors[9 + groups_mlp]
    every_block = lax.all_gather(blocks_low[None], "mlp", axis=0, tiled=True)
    attention_weights = every_block[:, 0]
    up_weight = every_block[:, 1]
    down_weight = every_block[:, 2]
    up_bias = up_rows.reshape(-1)
    inputs = tokens.astype(jnp.float32)
    norm_one, norm_one_back = jax.vjp(layer_norm, inputs, vectors[0], vectors[1])
    norm_one_low = norm_one.astype(jnp.bfloat16)
    query_lin = (
        jnp.dot(norm_one_low, attention_weights[0], preferred_element_type=jnp.float32) + vectors[2]
    )
    key_lin = (
        jnp.dot(norm_one_low, attention_weights[1], preferred_element_type=jnp.float32) + vectors[3]
    )
    value_low = (
        jnp.dot(norm_one_low, attention_weights[2], preferred_element_type=jnp.float32) + vectors[4]
    ).astype(jnp.bfloat16)
    rows_pos, cols_pos = patch_positions(segment, grid_height, grid_width, patch_rows, patch_cols)

    def rotary_map(flat_values, freq_values):
        return rotate_pairs(flat_values, freq_values, rows_pos, cols_pos)

    query_rot, query_back = jax.vjp(rotary_map, query_lin, freq_row)
    key_rot, key_back = jax.vjp(rotary_map, key_lin, freq_row)
    query_heads = heads_first(query_rot.astype(jnp.bfloat16))
    key_heads = heads_first(key_rot.astype(jnp.bfloat16))
    value_heads = heads_first(value_low)
    same_image = segment[:, None] == segment[None, :]
    score_scale = 1.0 / math.sqrt(model_width // HEADS)

    def head_scores(query_head, key_head):
        scores = jnp.dot(query_head, key_head.T, preferred_element_type=jnp.float32) * score_scale
        return jnp.where(same_image, scores, MASKED_SCORE)

    def head_forward(pieces):
        query_head, key_head, value_head = pieces
        scores = head_scores(query_head, key_head)
        row_peak = jnp.max(scores, axis=1, keepdims=True)
        exponent = jnp.exp(scores - row_peak)
        row_total = jnp.sum(exponent, axis=1, keepdims=True)
        weights_low = (exponent / row_total).astype(jnp.bfloat16)
        attended = jnp.dot(weights_low, value_head, preferred_element_type=jnp.float32)
        return (attended, (row_peak + jnp.log(row_total))[:, 0])

    attended_heads, log_totals = lax.map(head_forward, (query_heads, key_heads, value_heads))
    attended_low = tokens_first(attended_heads).astype(jnp.bfloat16)
    branch_one = (
        jnp.dot(attended_low, attention_weights[3], preferred_element_type=jnp.float32) + vectors[5]
    )
    middle = inputs + branch_one
    norm_two, norm_two_back = jax.vjp(layer_norm, middle, vectors[6], vectors[7])
    norm_two_low = norm_two.astype(jnp.bfloat16)
    pre_act = (
        jnp.einsum(
            "td,mde->tme", norm_two_low, up_weight, preferred_element_type=jnp.float32
        ).reshape(rows_here, -1)
        + up_bias
    )
    activation, gelu_back = jax.vjp(exact_gelu, pre_act)
    activation_blocks = activation.astype(jnp.bfloat16).reshape(rows_here, groups_mlp, -1)
    branch_two = (
        jnp.einsum(
            "tme,med->td", activation_blocks, down_weight, preferred_element_type=jnp.float32
        )
        + down_bias
    )
    grad_act = jnp.einsum(
        "td,med->tme", cotangent, down_weight, preferred_element_type=jnp.float32
    ).reshape(rows_here, -1)
    grad_down = jnp.einsum(
        "tme,td->med", activation_blocks, cotangent, preferred_element_type=jnp.float32
    )
    grad_pre_blocks = gelu_back(grad_act)[0].astype(jnp.bfloat16).reshape(rows_here, groups_mlp, -1)
    grad_up = jnp.einsum(
        "td,tme->mde", norm_two_low, grad_pre_blocks, preferred_element_type=jnp.float32
    )
    up_grad_rows = jnp.sum(grad_pre_blocks, axis=0, dtype=jnp.float32)
    grad_norm_two = jnp.einsum(
        "tme,mde->td", grad_pre_blocks, up_weight, preferred_element_type=jnp.float32
    )
    output_low = (middle + branch_two).astype(jnp.bfloat16)
    grad_middle_norm, grad_gain_two, grad_shift_two = norm_two_back(grad_norm_two)
    grad_middle = cotangent.astype(jnp.float32) + grad_middle_norm
    grad_branch_low = grad_middle.astype(jnp.bfloat16)
    grad_out_bias = jnp.sum(grad_branch_low, axis=0, dtype=jnp.float32)
    grad_out_weight = jnp.dot(attended_low.T, grad_branch_low, preferred_element_type=jnp.float32)
    grad_attended_low = jnp.dot(
        grad_branch_low, attention_weights[3].T, preferred_element_type=jnp.float32
    ).astype(jnp.bfloat16)

    def head_backward(pieces):
        query_head, key_head, value_head, grad_head, log_total = pieces
        scores = head_scores(query_head, key_head)
        probs = jnp.exp(scores - log_total[:, None])
        grad_probs = jnp.dot(grad_head, value_head.T, preferred_element_type=jnp.float32)
        inner = jnp.sum(probs * grad_probs, axis=1, keepdims=True)
        grad_scores = (probs * (grad_probs - inner)).astype(jnp.bfloat16)
        grad_query = (
            jnp.dot(grad_scores, key_head, preferred_element_type=jnp.float32) * score_scale
        )
        grad_key = (
            jnp.dot(grad_scores.T, query_head, preferred_element_type=jnp.float32) * score_scale
        )
        grad_value = jnp.dot(
            probs.astype(jnp.bfloat16).T, grad_head, preferred_element_type=jnp.float32
        )
        return (grad_query, grad_key, grad_value)

    grad_queries, grad_keys, grad_values = lax.map(
        head_backward,
        (query_heads, key_heads, value_heads, heads_first(grad_attended_low), log_totals),
    )
    grad_query_lin, grad_freq_query = query_back(tokens_first(grad_queries))
    grad_key_lin, grad_freq_key = key_back(tokens_first(grad_keys))
    grad_query_low = grad_query_lin.astype(jnp.bfloat16)
    grad_key_low = grad_key_lin.astype(jnp.bfloat16)
    grad_value_low = tokens_first(grad_values).astype(jnp.bfloat16)
    grad_query_weight = jnp.dot(norm_one_low.T, grad_query_low, preferred_element_type=jnp.float32)
    grad_key_weight = jnp.dot(norm_one_low.T, grad_key_low, preferred_element_type=jnp.float32)
    grad_value_weight = jnp.dot(norm_one_low.T, grad_value_low, preferred_element_type=jnp.float32)
    grad_norm_one = jnp.dot(
        grad_query_low, attention_weights[0].T, preferred_element_type=jnp.float32
    )
    grad_norm_one = grad_norm_one + jnp.dot(
        grad_key_low, attention_weights[1].T, preferred_element_type=jnp.float32
    )
    grad_norm_one = grad_norm_one + jnp.dot(
        grad_value_low, attention_weights[2].T, preferred_element_type=jnp.float32
    )
    grad_input_norm, grad_gain_one, grad_shift_one = norm_one_back(grad_norm_one)
    input_grad = grad_middle + grad_input_norm
    head_rows = jnp.stack(
        [
            grad_gain_one,
            grad_shift_one,
            jnp.sum(grad_query_low, axis=0, dtype=jnp.float32),
            jnp.sum(grad_key_low, axis=0, dtype=jnp.float32),
            jnp.sum(grad_value_low, axis=0, dtype=jnp.float32),
            grad_out_bias,
            grad_gain_two,
            grad_shift_two,
        ]
    )
    tail_rows = jnp.stack(
        [jnp.sum(cotangent, axis=0, dtype=jnp.float32), grad_freq_query + grad_freq_key]
    )
    local_vectors = jnp.concatenate([head_rows, up_grad_rows, tail_rows], axis=0)
    vector_sum = lax.psum(local_vectors, ("dp", "mlp"))
    attention_grads = jnp.stack(
        [grad_query_weight, grad_key_weight, grad_value_weight, grad_out_weight]
    )
    attention_share, up_share, down_share = (
        lax.psum_scatter(
            attention_grads.astype(jnp.bfloat16), "mlp", scatter_dimension=0, tiled=True
        ).astype(jnp.float32),
        lax.psum_scatter(
            grad_up.astype(jnp.bfloat16), "mlp", scatter_dimension=0, tiled=True
        ).astype(jnp.float32),
        lax.psum_scatter(
            grad_down.astype(jnp.bfloat16), "mlp", scatter_dimension=0, tiled=True
        ).astype(jnp.float32),
    )
    grad_stack = jnp.concatenate([attention_share, up_share, down_share], axis=0)
    reduced = lax.psum(grad_stack, "dp")
    block_kind = jnp.sum(jnp.where(holds_block, jnp.arange(3, dtype=jnp.int32), 0))
    owns_block = jnp.any(holds_block)
    gradient = jnp.take(reduced, block_kind, axis=0)
    decay_matrix = decays[0]
    left_old = left_slots[0, 0]
    right_old = right_slots[0, 0]
    master_old = master_slots[0, 0]
    left_next = decay_matrix * left_old + (1.0 - decay_matrix) * jnp.dot(
        gradient, gradient.T, precision=lax.Precision.HIGHEST
    )
    right_next = decay_matrix * right_old + (1.0 - decay_matrix) * jnp.dot(
        gradient.T, gradient, precision=lax.Precision.HIGHEST
    )
    direction = jnp.dot(
        jnp.dot(left_roots[0, 0], gradient, precision=lax.Precision.HIGHEST),
        right_roots[0, 0],
        precision=lax.Precision.HIGHEST,
    )
    normed_step = direction * lax.rsqrt(jnp.mean(direction * direction) + GRAFT_EPSILON)
    master_next = master_old - RATE_MATRIX * normed_step
    slot_grad = jnp.where(owns_block, gradient, 0.0)[None, None]
    left_out = jnp.where(owns_block, left_next, left_old)[None, None]
    right_out = jnp.where(owns_block, right_next, right_old)[None, None]
    master_out = jnp.where(owns_block, master_next, master_old)[None, None]
    share_width = model_width // groups_mlp

    def own_columns(table):
        return lax.dynamic_slice_in_dim(table, mlp_index * share_width, share_width, 1)

    grad_share = own_columns(vector_sum)
    moment_old = own_columns(vector_moments)
    vector_old = own_columns(vectors)
    decay_vector = decays[1]
    moment_next = decay_vector * moment_old + (1.0 - decay_vector) * grad_share * grad_share
    vector_next = vector_old - RATE_VECTOR * grad_share / (jnp.sqrt(moment_next) + STEP_EPSILON)
    return (
        output_low,
        input_grad,
        slot_grad,
        left_out,
        right_out,
        master_out,
        grad_share,
        moment_next,
        vector_next,
    )


def solution(mesh):
    placed = (
        P(("dp", "mlp"), None),
        P(("dp", "mlp"), None),
        P(),
        P(),
        P(),
        P(),
        P("dp", "mlp", None, None),
        P("dp", "mlp", None, None),
        P("dp", "mlp", None, None),
        P("dp", "mlp", None, None),
        P("dp", "mlp", None, None),
        P(("dp", "mlp")),
        P(("dp", "mlp")),
        P(("dp", "mlp")),
        P(("dp", "mlp")),
        P(("dp", "mlp")),
    )
    return jax.shard_map(
        local,
        mesh=mesh,
        in_specs=placed,
        out_specs=(
            P(("dp", "mlp"), None),
            P(("dp", "mlp"), None),
            P("dp", "mlp", None, None),
            P("dp", "mlp", None, None),
            P("dp", "mlp", None, None),
            P("dp", "mlp", None, None),
            P(None, "mlp"),
            P(None, "mlp"),
            P(None, "mlp"),
        ),
        check_vma=False,
    )
```

profile of v0, /device:TPU:0, one launch (start us, length us, event | category | flops | bytes accessed | tf_op | source)
XLA Modules:
  0.0 1202.3 jit_solution(14143546167382789815)
XLA Ops:
  14.0 278.3 %all-reduce.12 = bf16[3,768,768]{2,1,0:T(8,128)(2,1)} all-reduce(f32[3,768,768]{2,1,0:T(8,128)} %broadcast_select_fusion), channel_id=1, replica_groups=mesh['dp'=8,'mlp'=4] {'dp'}, use_global_device_ids=true, to_apply=%region_2.3 | all-reduce | flops 1769472 | bytes 10616832 | tf_op jit(solution)/shard_map/psum | solution.py:92
  303.2 78.7 %all-gather.3.cloned.1.call-done = bf16[12,768,768]{2,1,0:T(8,128)(2,1)} async-done(((bf16[3,768,768]{2,1,0:T(8,128)(2,1)}), bf16[12,768,768]{2,1,0:T(8,128)(2,1)}) %all-gather.3.cloned.1.call-update) | async-done | bytes 14155792 | tf_op jit(solution)/shard_map/all_gather | solution.py:97
  393.6 7.7 subtract_convert_fusion
  421.8 85.7 %while.32 = (s32[]{:T(128)}, bf16[12,1024,64]{1,2,0:T(8,128)(2,1)}, f32[12,1024]{1,0:T(8,128)}, bf16[12,1024,64]{2,1,0:T(8,128)(2,1)}, bf16[12,1024,64]{2,1,0:T(...) while((s32[]{:T(128)}, bf16[12,1024,64]{1,2,0:T(8,128)(2,1)}, ...), condition=%wide.region_8.9_spmd.clone.clone, body=%wide.region_5.8_spmd.clone.sunk.clone | while | flops 284163072 | bytes 13695065 | solution.py:141
  507.5 10.2 fusion.64
  517.7 12.7 %copy.133 = f32[1024,3072]{1,0:T(8,128)} copy(f32[1024,3072]{0,1:T(8,128)} %bitcast.277) | data formatting | bytes 25165824 | tf_op jit(solution)/shard_map/reshape | solution.py:165
  544.0 40.9 %convert_reduce_fusion = (f32[3072]{0:T(1024)}, bf16[1024,3072]{1,0:T(8,128)(2,1)}, f32[1024,3072]{1,0:T(8,128)}, f32[1024,3072]{1,0:T(8,128)}) fusion(f32[1024,3072]{1,0:T(8,128)S(1)} %copy-done.14, f32[3072]{0:T(1024)S(1)} %add.236, bf16[3072,768]{1,0:T(8,128)(2,1)} %bitcast.289, f32[1024,768]{0,1:T(8,128)S(1)} %get-tuple-element.370, ...), kind=kOutput, calls=%fused_computation.58 | convolution fusion | flops 5071696896 | bytes 51943424 | tf_op jit(solution)/shard_map/td,mde->tme/dot_general | solution.py:150
  584.9 12.8 %multiply_convert_fusion.1 = bf16[1024,3072]{1,0:T(8,128)(2,1)} fusion(f32[1024,3072]{1,0:T(8,128)} %get-tuple-element.336, f32[1024,3072]{1,0:T(8,128)} %get-tuple-element.371, f32[3072]{0:T(1024)S(1)} %add.236), kind=kLoop, calls=%fused_computation.60 | loop fusion | flops 12582912 | bytes 31469568 | tf_op jit(solution)/shard_map/convert_element_type | solution.py:156
  597.8 8.6 copy.137
  606.4 9.0 convolution_convert_fusion
  618.0 8.8 copy.138
  626.8 9.9 fusion.141
  655.9 10.4 convert_bitcast_fusion
  667.0 159.3 %while.33 = (s32[]{:T(128)}, f32[12,1024,64]{1,2,0:T(8,128)}, f32[12,1024,64]{1,2,0:T(8,128)}, bf16[12,1024,64]{1,2,0:T(8,128)(2,1)}, bf16[12,1024,64]{2,1,0:T(8...) while((s32[]{:T(128)}, f32[12,1024,64]{1,2,0:T(8,128)}, ...), condition=%wide.region_15.16_spmd.clone.clone, body=%wide.region_13.15_spmd.clone.sunk.clone | while | flops 681704448 | bytes 34112624 | solution.py:205
  826.3 12.0 multiply_add_fusion.1
  840.7 7.8 multiply_add_fusion
  860.6 48.4 %reduce-scatter.4.cloned.1.call-done = bf16[1,768,768]{2,1,0:T(8,128)(2,1)} async-done(((bf16[4,768,768]{2,1,0:T(8,128)(2,1)}), bf16[1,768,768]{2,1,0:T(8,128)(2,1)}) %reduce-scatter.4.cloned.1.call-update) | async-done | bytes 1179664 | tf_op jit(solution)/shard_map/reduce_scatter | solution.py:249
  919.4 10.5 fusion.75
  955.9 45.1 %psum.23 = f32[14,768]{1,0:T(8,128)S(1)} all-reduce(f32[14,768]{1,0:T(8,128)S(1)} %concatenate.21), channel_id=1, replica_groups=mesh['dp'=8,'mlp'=4] {'dp','mlp'}, use_global_device_ids=true, to_apply=%region_39.40 | all-reduce | flops 10752 | bytes 86016 | tf_op jit(solution)/shard_map/psum | solution.py:244
  1003.1 143.9 %all-reduce.11.cloned.1.call-done = f32[3,768,768]{2,1,0:T(8,128)} async-done(((f32[3,768,768]{2,1,0:T(8,128)}), f32[3,768,768]{2,1,0:T(8,128)}) %all-reduce.11.cloned.1.call-update) | async-done | bytes 7077904 | tf_op jit(solution)/shard_map/psum | solution.py:260
  1147.1 13.6 %fusion.79 = f32[768,768]{1,0:T(8,128)S(1)} fusion(f32[1,1,768,768]{3,2,1,0:T(8,128)} %param.29, f32[3,768,768]{2,1,0:T(8,128)} %all-reduce.11.cloned.1.call-done, s32[]{:T(128)S(6)} %select_n.95, pred[]{:T(512)S(6)} %and.13), kind=kOutput, calls=%fused_computation.124 | convolution fusion | flops 5436407808 | bytes 7077893 | tf_op jit(solution)/shard_map/dot_general | solution.py:275
  1160.7 8.7 multiply_reduce_fusion.4
  1177.5 8.9 fusion.84
  1186.4 9.2 fusion.82
  (355 shorter events, 387.2 us)
Async XLA Ops:
  7.2 1153.5 %copy-start = (f32[1,1,768,768]{3,2,1,0:T(8,128)S(1)}, f32[1,1,768,768]{3,2,1,0:T(8,128)}, u32[]{:S(2)}) copy-start(f32[1,1,768,768]{3,2,1,0:T(8,128)} %param.30) | copy-start | bytes 7077892
  7.2 374.6 %all-gather.3.cloned.1.call-start = ((), (), s32[]{:S(2)}) async-start(), calls=%async_computation.7 | async-start | bytes 17694720 | tf_op jit(solution)/shard_map/all_gather | solution.py:97
  292.3 568.3 %reduce-scatter.8.cloned.1.call-start = ((), (), s32[]{:S(2)}) async-start(), calls=%async_computation.5 | async-start | bytes 5898240 | tf_op jit(solution)/shard_map/reduce_scatter | solution.py:255
  294.8 8.3 copy-start.51
  297.5 96.0 %copy-start.28 = (f32[12,32]{1,0:T(8,128)}, f32[12,32]{1,0:T(8,128)S(1)}, u32[]{:S(2)}) copy-start(f32[12,32]{1,0:T(8,128)S(1)} %mul.390) | copy-start | bytes 4612
  297.6 95.9 %copy-start.30 = (f32[12,32]{1,0:T(8,128)}, f32[12,32]{1,0:T(8,128)S(1)}, u32[]{:S(2)}) copy-start(f32[12,32]{1,0:T(8,128)S(1)} %mul.385) | copy-start | bytes 4612
  298.4 114.8 %copy-start.40 = (f32[768]{0:T(1024)}, f32[768]{0:T(1024)S(1)}, u32[]{:S(2)}) copy-start(f32[768]{0:T(1024)S(1)} %get-tuple-element.290) | copy-start | bytes 9220
  298.4 114.8 %copy-start.48 = (f32[768]{0:T(1024)}, f32[768]{0:T(1024)S(1)}, u32[]{:S(2)}) copy-start(f32[768]{0:T(1024)S(1)} %get-tuple-element.289) | copy-start | bytes 9220
  300.4 112.8 %copy-start.32 = (f32[1024]{0:T(1024)}, f32[1024]{0:T(1024)S(1)}, u32[]{:S(2)}) copy-start(f32[1024]{0:T(1024)S(1)} %broadcast_multiply_fusion.1) | copy-start | bytes 12292
  302.5 110.7 %copy-start.42 = (f32[1024]{0:T(1024)}, f32[1024]{0:T(1024)S(1)}, u32[]{:S(2)}) copy-start(f32[1024]{0:T(1024)S(1)} %fusion.118) | copy-start | bytes 12292
  303.1 90.4 %copy-start.34 = (f32[1024]{0:T(1024)}, f32[1024]{0:T(1024)S(1)}, u32[]{:S(2)}) copy-start(f32[1024]{0:T(1024)S(1)} %get-tuple-element.377) | copy-start | bytes 12292
  303.1 90.4 %copy-start.36 = (f32[1024]{0:T(1024)}, f32[1024]{0:T(1024)S(1)}, u32[]{:S(2)}) copy-start(f32[1024]{0:T(1024)S(1)} %get-tuple-element.378) | copy-start | bytes 12292
  541.0 43.9 %copy-start.4 = (f32[1024,768]{0,1:T(8,128)}, f32[1024,768]{0,1:T(8,128)S(1)}, u32[]{:S(2)}) copy-start(f32[1024,768]{0,1:T(8,128)S(1)} %get-tuple-element.370) | copy-start | bytes 9437188
  615.4 245.2 %reduce-scatter.6.cloned.1.call-start = ((), (), s32[]{:S(2)}) async-start(), calls=%async_computation.4 | async-start | bytes 5898240 | tf_op jit(solution)/shard_map/reduce_scatter | solution.py:252
  666.3 242.7 %reduce-scatter.4.cloned.1.call-start = ((), (), s32[]{:S(2)}) async-start(), calls=%async_computation.3 | async-start | bytes 5898240 | tf_op jit(solution)/shard_map/reduce_scatter | solution.py:249
  667.0 159.3 %copy-start.29 = (f32[12,32]{1,0:T(8,128)S(1)}, f32[12,32]{1,0:T(8,128)}, u32[]{:S(2)}) copy-start(f32[12,32]{1,0:T(8,128)} %copy-done.28) | copy-start | bytes 4612
  667.0 159.3 %copy-start.31 = (f32[12,32]{1,0:T(8,128)S(1)}, f32[12,32]{1,0:T(8,128)}, u32[]{:S(2)}) copy-start(f32[12,32]{1,0:T(8,128)} %copy-done.30) | copy-start | bytes 4612
  667.0 159.3 %copy-start.35 = (f32[1024]{0:T(1024)S(1)}, f32[1024]{0:T(1024)}, u32[]{:S(2)}) copy-start(f32[1024]{0:T(1024)} %copy-done.34) | copy-start | bytes 12292
  667.0 159.3 %copy-start.37 = (f32[1024]{0:T(1024)S(1)}, f32[1024]{0:T(1024)}, u32[]{:S(2)}) copy-start(f32[1024]{0:T(1024)} %copy-done.36) | copy-start | bytes 12292
  826.3 12.3 %copy-start.18 = (f32[12,1024,64]{1,2,0:T(8,128)S(1)}, f32[12,1024,64]{1,2,0:T(8,128)}, u32[]{:S(2)}) copy-start(f32[12,1024,64]{1,2,0:T(8,128)} %get-tuple-element.104) | copy-start | bytes 9437188
  838.5 17.7 %copy-start.25 = (bf16[1024,12,64]{0,2,1:T(8,128)(2,1)}, bf16[1024,12,64]{0,2,1:T(8,128)(2,1)S(1)}, u32[]{:S(2)}) copy-start(bf16[1024,12,64]{0,2,1:T(8,128)(2,1)S(1)} %get-tuple-element.342) | copy-start | bytes 4718596
  860.3 286.7 %all-reduce.11.cloned.1.call-start = ((), (), s32[]{:S(2)}) async-start(), calls=%async_computation.6 | async-start | bytes 14155776 | tf_op jit(solution)/shard_map/psum | solution.py:260
  951.0 50.0 %copy-start.39 = (f32[14,768]{1,0:T(8,128)S(1)}, f32[14,768]{1,0:T(8,128)}, u32[]{:S(2)}) copy-start(f32[14,768]{1,0:T(8,128)} %param.22) | copy-start | bytes 129028
  1177.5 8.9 copy-start.56
  (39 other events, 130.4 us)
Sparse Core Ops, SparseCore 0:
  292.4 89.3 all-gather.2
  615.5 47.9 reduce-scatter.7
  666.4 48.3 reduce-scatter.5
  860.4 48.5 reduce-scatter.3
  914.5 232.5 all-reduce.10
where the time goes:
time: 1220 us; the launch traced here: 1200 us
  matrix products  359 us (29%)
  blocking collectives  323 us (26%)
  waiting for transfers between devices  271 us (22%)
  local copies, waits for them, and re-layouts  115 us (9%)
  other arithmetic  115 us (9%)
  between operations  18.4 us (2%)
    psum x1, blocking collectives, local(): blocks = lax.psum(owned_blocks, 'dp')  278 us
    psum x1, waiting for transfers between devices, local(): reduced = lax.psum(grad_stack, 'dp')  144 us
    all_gather x1, waiting for transfers between devices, local(): every_block = lax.all_gather(blocks_low[None], 'mlp', axis=0, tiled=True)  78.7 us
    dot_general x24, matrix products, head_scores(): jnp.dot(query_head, key_head.T, preferred_element_type=jnp.float32)  52.2 us
    reduce_scatter x1, waiting for transfers between devices, local(): lax.psum_scatter(attention_grads.astype(jnp.bfloat16), 'mlp', scatter_dim...  48.4 us
    psum x1, blocking collectives, local(): vector_sum = lax.psum(local_vectors, ('dp', 'mlp'))  45.1 us
    dot_general x1, matrix products, local(): jnp.einsum('td,mde->tme', norm_two_low, up_weight, preferred_element_type...  40.9 us
    dot_general x12, matrix products, head_forward(): jnp.dot(weights_low, value_head, preferred_element_type=jnp.float32)  35.5 us
  transfers between devices with their start and end apart: 5, of which 3 were waited for; matrix products, arithmetic and copies ran while one was open for 24% of the time, Pallas kernels for 0%

commit v1 on v0

--- a/solution.py
+++ b/solution.py
@@ -89,7 +89,12 @@
     owner_row = jnp.take(owner, mlp_index, axis=0)
     holds_block = owner_row == dp_index
     owned_blocks = jnp.where(holds_block[:, None, None], master_slots[0, 0][None], 0.0)
-    blocks = lax.psum(owned_blocks, "dp")
+    lanes = lax.axis_size("dp")
+    blocks, fresh = (owned_blocks, 0)
+    while 1 << fresh < lanes:
+        part_now = lax.ppermute(blocks, "dp", [(j0, j0 ^ 1 << fresh) for j0 in range(lanes)])
+        blocks = blocks + part_now
+        fresh = fresh + 1
     blocks_low = blocks.astype(jnp.bfloat16)
     up_rows = vectors[8 : 8 + groups_mlp]
     down_bias = vectors[8 + groups_mlp]

time: 1220 us -> 1560 us (1.28)
  waiting for transfers between devices: 271 us -> 880 us
  blocking collectives: 323 us -> 45.1 us
    ppermute x0 -> x3, waiting for transfers between devices: none -> 607 us  [local(): lax.ppermute(blocks, 'dp', [(j0, j0 ^ 1 << fresh) for j0 in range(lanes)])]
    psum x1 -> x0, blocking collectives: 278 us -> none  [local(): blocks = lax.psum(owned_blocks, 'dp')]
    unnamed x121 -> x125, local copies, waits for them, and re-layouts: 33.5 us -> 35.6 us
  transfers between devices with their start and end apart: 5 -> 8, of which waited for: 3 -> 6; matrix products, arithmetic and copies ran while one was open for 24% -> 18% of each run, Pallas kernels for 0% -> 0%
where the time goes in v1:
time: 1560 us
  waiting for transfers between devices  880 us (56%)
  matrix products  359 us (23%)
  other arithmetic  127 us (8%)
  local copies, waits for them, and re-layouts  117 us (8%)
  blocking collectives  45.1 us (3%)
  between operations  18.4 us (1%)
    ppermute x3, waiting for transfers between devices, local(): lax.ppermute(blocks, 'dp', [(j0, j0 ^ 1 << fresh) for j0 in range(lanes)])  607 us
    psum x1, waiting for transfers between devices, local(): reduced = lax.psum(grad_stack, 'dp')  144 us
    all_gather x1, waiting for transfers between devices, local(): every_block = lax.all_gather(blocks_low[None], 'mlp', axis=0, tiled=True)  80.6 us
    dot_general x24, matrix products, head_scores(): jnp.dot(query_head, key_head.T, preferred_element_type=jnp.float32)  52.2 us
    reduce_scatter x1, waiting for transfers between devices, local(): lax.psum_scatter(attention_grads.astype(jnp.bfloat16), 'mlp', scatter_dim...  48.4 us
    psum x1, blocking collectives, local(): vector_sum = lax.psum(local_vectors, ('dp', 'mlp'))  45.1 us
    dot_general x1, matrix products, local(): jnp.einsum('td,mde->tme', norm_two_low, up_weight, preferred_element_type...  40.9 us
    unnamed x125, local copies, waits for them, and re-layouts  35.6 us
  transfers between devices with their start and end apart: 8, of which 6 were waited for; matrix products, arithmetic and copies ran while one was open for 18% of the time, Pallas kernels for 0%

profile of v1, /device:TPU:0, one launch (start us, length us, event | category | flops | bytes accessed | tf_op | source)
XLA Modules:
  0.0 1555.9 jit_solution(6238470963558493772)
XLA Ops:
  14.2 152.4 %collective-permute-done = f32[3,768,768]{2,1,0:T(8,128)S(1)} collective-permute-done((f32[3,768,768]{2,1,0:T(8,128)S(1)}, f32[3,768,768]{2,1,0:T(8,128)S(1)}, u32[]{:S(2)}, u32[]{:S(2)}) %collective-permute-start) | collective-permute-done | bytes 7077920 | tf_op jit(solution)/shard_map/ppermute | solution.py:95
  171.2 151.8 %collective-permute-done.1 = f32[3,768,768]{2,1,0:T(8,128)} collective-permute-done((f32[3,768,768]{2,1,0:T(8,128)S(1)}, f32[3,768,768]{2,1,0:T(8,128)}, u32[]{:S(2)}, u32[]{:S(2)}) %collective-permute-start.1) | collective-permute-done | bytes 7077920 | tf_op jit(solution)/shard_map/ppermute | solution.py:95
  323.0 9.3 fusion.161
  334.9 302.9 %collective-permute-done.2 = f32[3,768,768]{2,1,0:T(8,128)S(1)} collective-permute-done((f32[3,768,768]{2,1,0:T(8,128)}, f32[3,768,768]{2,1,0:T(8,128)S(1)}, u32[]{:S(2)}, u32[]{:S(2)}) %collective-permute-start.2) | collective-permute-done | bytes 7077920 | tf_op jit(solution)/shard_map/ppermute | solution.py:95
  654.7 80.6 %all-gather.3.cloned.1.call-done = bf16[12,768,768]{2,1,0:T(8,128)(2,1)} async-done(((bf16[3,768,768]{2,1,0:T(8,128)(2,1)}), bf16[12,768,768]{2,1,0:T(8,128)(2,1)}) %all-gather.3.cloned.1.call-update) | async-done | bytes 14155792 | tf_op jit(solution)/shard_map/all_gather | solution.py:102
  775.3 85.7 %while.32 = (s32[]{:T(128)}, bf16[12,1024,64]{1,2,0:T(8,128)(2,1)}, f32[12,1024]{1,0:T(8,128)}, bf16[12,1024,64]{2,1,0:T(8,128)(2,1)}, bf16[12,1024,64]{2,1,0:T(...) while((s32[]{:T(128)}, bf16[12,1024,64]{1,2,0:T(8,128)(2,1)}, ...), condition=%wide.region_7.8_spmd.clone.clone, body=%wide.region_4.7_spmd.clone.sunk.clone | while | flops 284163072 | bytes 13695065 | solution.py:146
  861.0 10.2 fusion.64
  871.2 12.7 copy.133
  897.5 40.9 %convert_reduce_fusion = (f32[3072]{0:T(1024)}, bf16[1024,3072]{1,0:T(8,128)(2,1)}, f32[1024,3072]{1,0:T(8,128)}, f32[1024,3072]{1,0:T(8,128)}) fusion(f32[1024,3072]{1,0:T(8,128)S(1)} %copy-done.16, f32[3072]{0:T(1024)S(1)} %add.246, bf16[3072,768]{1,0:T(8,128)(2,1)} %bitcast.291, f32[1024,768]{0,1:T(8,128)S(1)} %get-tuple-element.370, ...), kind=kOutput, calls=%fused_computation.58 | convolution fusion | flops 5071696896 | bytes 51943424 | tf_op jit(solution)/shard_map/td,mde->tme/dot_general | solution.py:155
  938.5 12.8 multiply_convert_fusion.1
  959.9 9.0 convolution_convert_fusion
  971.6 8.8 copy.138
  980.3 9.9 fusion.142
  1009.4 10.4 convert_bitcast_fusion
  1020.5 159.3 %while.33 = (s32[]{:T(128)}, f32[12,1024,64]{1,2,0:T(8,128)}, f32[12,1024,64]{1,2,0:T(8,128)}, bf16[12,1024,64]{1,2,0:T(8,128)(2,1)}, bf16[12,1024,64]{2,1,0:T(8...) while((s32[]{:T(128)}, f32[12,1024,64]{1,2,0:T(8,128)}, ...), condition=%wide.region_14.15_spmd.clone.clone, body=%wide.region_12.14_spmd.clone.sunk.clone | while | flops 681704448 | bytes 34112624 | solution.py:210
  1179.8 12.0 multiply_add_fusion.1
  1214.2 48.4 %reduce-scatter.4.cloned.1.call-done = bf16[1,768,768]{2,1,0:T(8,128)(2,1)} async-done(((bf16[4,768,768]{2,1,0:T(8,128)(2,1)}), bf16[1,768,768]{2,1,0:T(8,128)(2,1)}) %reduce-scatter.4.cloned.1.call-update) | async-done | bytes 1179664 | tf_op jit(solution)/shard_map/reduce_scatter | solution.py:254
  1272.9 10.5 fusion.75
  1309.4 45.1 %psum.15 = f32[14,768]{1,0:T(8,128)S(1)} all-reduce(f32[14,768]{1,0:T(8,128)S(1)} %concatenate.21), channel_id=1, replica_groups=mesh['dp'=8,'mlp'=4] {'dp','mlp'}, use_global_device_ids=true, to_apply=%region_38.39 | all-reduce | flops 10752 | bytes 86016 | tf_op jit(solution)/shard_map/psum | solution.py:249
  1356.7 143.9 %all-reduce.10.cloned.1.call-done = f32[3,768,768]{2,1,0:T(8,128)} async-done(((f32[3,768,768]{2,1,0:T(8,128)}), f32[3,768,768]{2,1,0:T(8,128)}) %all-reduce.10.cloned.1.call-update) | async-done | bytes 7077904 | tf_op jit(solution)/shard_map/psum | solution.py:265
  1500.6 13.6 fusion.79
  1514.2 8.7 multiply_reduce_fusion.4
  1531.0 8.9 fusion.84
  1539.9 9.2 fusion.82
  (367 shorter events, 424.8 us)
Async XLA Ops:
  7.2 1507.0 %copy-start = (f32[1,1,768,768]{3,2,1,0:T(8,128)S(1)}, f32[1,1,768,768]{3,2,1,0:T(8,128)}, u32[]{:S(2)}) copy-start(f32[1,1,768,768]{3,2,1,0:T(8,128)} %param.30) | copy-start | bytes 7077892
  7.2 728.1 %all-gather.3.cloned.1.call-start = ((), (), s32[]{:S(2)}) async-start(), calls=%async_computation.7 | async-start | bytes 17694720 | tf_op jit(solution)/shard_map/all_gather | solution.py:102
  8.8 157.8 %copy-start.4 = (f32[1,1,768,768]{3,2,1,0:T(8,128)S(1)}, f32[1,1,768,768]{3,2,1,0:T(8,128)}, u32[]{:S(2)}) copy-start(f32[1,1,768,768]{3,2,1,0:T(8,128)} %param.26) | copy-start | bytes 7077892
  11.2 155.4 %collective-permute-start = (f32[3,768,768]{2,1,0:T(8,128)S(1)}, f32[3,768,768]{2,1,0:T(8,128)S(1)}, u32[]{:S(2)}, u32[]{:S(2)}) collective-permute-start(f32[3,768,768]{2,1,0:T(8,128)S(1)} %broadcast_select_fusion), channel_id=1, source_target_pairs={{0,4},{4,0},{8,12},{12,8},{16,20},{20,16},{24,28},{28,24},{1,5},{5... | collective-permute-start | bytes 21233672 | tf_op jit(solution)/shard_map/ppermute | solution.py:95
  169.4 153.6 %collective-permute-start.1 = (f32[3,768,768]{2,1,0:T(8,128)S(1)}, f32[3,768,768]{2,1,0:T(8,128)}, u32[]{:S(2)}, u32[]{:S(2)}) collective-permute-start(f32[3,768,768]{2,1,0:T(8,128)S(1)} %fusion.114), channel_id=1, source_target_pairs={{0,8},{4,12},{8,0},{12,4},{16,24},{20,28},{24,16},{28,20},{1,9},{5... | collective-permute-start | bytes 21233672 | tf_op jit(solution)/shard_map/ppermute | solution.py:95
  332.4 305.5 %collective-permute-start.2 = (f32[3,768,768]{2,1,0:T(8,128)}, f32[3,768,768]{2,1,0:T(8,128)S(1)}, u32[]{:S(2)}, u32[]{:S(2)}) collective-permute-start(f32[3,768,768]{2,1,0:T(8,128)} %fusion.161), channel_id=1, source_target_pairs={{0,16},{4,20},{8,24},{12,28},{16,0},{20,4},{24,8},{28,12},{1,17},{... | collective-permute-start | bytes 21233672 | tf_op jit(solution)/shard_map/ppermute | solution.py:95
  643.3 570.8 %reduce-scatter.8.cloned.1.call-start = ((), (), s32[]{:S(2)}) async-start(), calls=%async_computation.5 | async-start | bytes 5898240 | tf_op jit(solution)/shard_map/reduce_scatter | solution.py:260
  649.1 97.9 %copy-start.30 = (f32[12,32]{1,0:T(8,128)}, f32[12,32]{1,0:T(8,128)S(1)}, u32[]{:S(2)}) copy-start(f32[12,32]{1,0:T(8,128)S(1)} %mul.390) | copy-start | bytes 4612
  649.2 97.8 %copy-start.32 = (f32[12,32]{1,0:T(8,128)}, f32[12,32]{1,0:T(8,128)S(1)}, u32[]{:S(2)}) copy-start(f32[12,32]{1,0:T(8,128)S(1)} %mul.385) | copy-start | bytes 4612
  650.0 116.7 %copy-start.42 = (f32[768]{0:T(1024)}, f32[768]{0:T(1024)S(1)}, u32[]{:S(2)}) copy-start(f32[768]{0:T(1024)S(1)} %get-tuple-element.290) | copy-start | bytes 9220
  650.0 116.7 %copy-start.50 = (f32[768]{0:T(1024)}, f32[768]{0:T(1024)S(1)}, u32[]{:S(2)}) copy-start(f32[768]{0:T(1024)S(1)} %get-tuple-element.289) | copy-start | bytes 9220
  651.9 114.8 %copy-start.34 = (f32[1024]{0:T(1024)}, f32[1024]{0:T(1024)S(1)}, u32[]{:S(2)}) copy-start(f32[1024]{0:T(1024)S(1)} %broadcast_multiply_fusion.1) | copy-start | bytes 12292
  654.1 112.6 %copy-start.44 = (f32[1024]{0:T(1024)}, f32[1024]{0:T(1024)S(1)}, u32[]{:S(2)}) copy-start(f32[1024]{0:T(1024)S(1)} %fusion.119) | copy-start | bytes 12292
  654.7 92.3 %copy-start.36 = (f32[1024]{0:T(1024)}, f32[1024]{0:T(1024)S(1)}, u32[]{:S(2)}) copy-start(f32[1024]{0:T(1024)S(1)} %get-tuple-element.377) | copy-start | bytes 12292
  654.7 92.3 %copy-start.38 = (f32[1024]{0:T(1024)}, f32[1024]{0:T(1024)S(1)}, u32[]{:S(2)}) copy-start(f32[1024]{0:T(1024)S(1)} %get-tuple-element.378) | copy-start | bytes 12292
  894.5 43.9 %copy-start.6 = (f32[1024,768]{0,1:T(8,128)}, f32[1024,768]{0,1:T(8,128)S(1)}, u32[]{:S(2)}) copy-start(f32[1024,768]{0,1:T(8,128)S(1)} %get-tuple-element.370) | copy-start | bytes 9437188
  968.9 245.2 %reduce-scatter.6.cloned.1.call-start = ((), (), s32[]{:S(2)}) async-start(), calls=%async_computation.4 | async-start | bytes 5898240 | tf_op jit(solution)/shard_map/reduce_scatter | solution.py:257
  1019.8 242.7 %reduce-scatter.4.cloned.1.call-start = ((), (), s32[]{:S(2)}) async-start(), calls=%async_computation.3 | async-start | bytes 5898240 | tf_op jit(solution)/shard_map/reduce_scatter | solution.py:254
  1020.5 159.3 %copy-start.31 = (f32[12,32]{1,0:T(8,128)S(1)}, f32[12,32]{1,0:T(8,128)}, u32[]{:S(2)}) copy-start(f32[12,32]{1,0:T(8,128)} %copy-done.30) | copy-start | bytes 4612
  1020.5 159.3 %copy-start.33 = (f32[12,32]{1,0:T(8,128)S(1)}, f32[12,32]{1,0:T(8,128)}, u32[]{:S(2)}) copy-start(f32[12,32]{1,0:T(8,128)} %copy-done.32) | copy-start | bytes 4612
  1020.5 159.3 %copy-start.37 = (f32[1024]{0:T(1024)S(1)}, f32[1024]{0:T(1024)}, u32[]{:S(2)}) copy-start(f32[1024]{0:T(1024)} %copy-done.36) | copy-start | bytes 12292
  1020.5 159.3 %copy-start.39 = (f32[1024]{0:T(1024)S(1)}, f32[1024]{0:T(1024)}, u32[]{:S(2)}) copy-start(f32[1024]{0:T(1024)} %copy-done.38) | copy-start | bytes 12292
  1213.8 286.7 %all-reduce.10.cloned.1.call-start = ((), (), s32[]{:S(2)}) async-start(), calls=%async_computation.6 | async-start | bytes 14155776 | tf_op jit(solution)/shard_map/psum | solution.py:265
  1304.6 50.0 %copy-start.41 = (f32[14,768]{1,0:T(8,128)S(1)}, f32[14,768]{1,0:T(8,128)}, u32[]{:S(2)}) copy-start(f32[14,768]{1,0:T(8,128)} %param.22) | copy-start | bytes 129028
  (44 other events, 180.2 us)
Sparse Core Ops, SparseCore 0:
  643.5 91.8 all-gather.2
  969.0 47.9 reduce-scatter.7
  1020.0 48.3 reduce-scatter.5
  1214.0 48.5 reduce-scatter.3
  1268.0 232.5 all-reduce.9
